TPU v7x, 256 devices: a whole 4x4x8 slice. The times are simulated.
256 devices in a mesh: pipe: 2 (over core), expert: 16 (over y, x), dp: 8 (over z).
Axes of the slice: x: 4, y: 4, z: 8, core: 2. Of those that a mesh axis runs over, the one named last changes fastest.
Arguments:
- tokens: bfloat16 [2048, 6144], P('expert'), may hold values from -6 to 6
- expert_ids: int32 [2048, 2], P('expert'), may hold values from 0 to 15, all different within a row; in each aligned block of 128 rows (0 to 127, 128 to 255, ...) at most 24 rows name the same one
- w_router: bfloat16 [6144, 16], replicated, may hold values from -0.078125 to 0.078125
- w_gate: bfloat16 [16, 6144, 4096], P('expert', None, ('pipe', 'dp')), may hold values from -0.078125 to 0.078125
- w_up: bfloat16 [16, 6144, 4096], P('expert', None, ('pipe', 'dp')), may hold values from -0.078125 to 0.078125
- w_down: bfloat16 [16, 4096, 6144], P('expert', ('pipe', 'dp')), may hold values from -0.125 to 0.125
Outputs:
- mixed: bfloat16 [2048, 6144], P('expert', ('pipe', 'dp'))
Inputs may be any that keep to these rules, and one draw needn't show every extreme that they name: `expert_ids`: in each aligned block of 128 tokens no expert is named by more than 24 of the block's choices, a bound that some block reaches; the two experts of a token differ.
All inputs are finite; a program needn't handle non-finite values.
Results may differ from a plain program's by a relative error of at most 0.018.
Values may be sent and summed in bfloat16 or wider, within the bound.
A program may use at most 64 MiB of HBM per device.

v0:
```python
import jax
import jax.numpy as jnp
from jax import lax
from jax.sharding import PartitionSpec as P


def slots_of(ids, experts):
    blocks = ids.shape[0]
    flat = ids.reshape(blocks, -1)
    onehot = (flat[:, :, None] == jnp.arange(experts, dtype=jnp.int32)[None, None, :]).astype(
        jnp.int32
    )
    before = jnp.cumsum(onehot, axis=1) - onehot
    slot = jnp.sum(before * onehot, axis=-1)
    return (flat, slot)


def dispatch(x_rows, id_rows, experts, capacity):
    count, width = x_rows.shape
    topk = id_rows.shape[1]
    flat, slot = slots_of(id_rows[None], experts)
    dest = flat[0] * capacity + slot[0]
    select = (jnp.arange(experts * capacity, dtype=jnp.int32)[:, None] == dest[None, :]).astype(
        jnp.bfloat16
    )
    repeated = jnp.repeat(x_rows, topk, axis=0)
    placed = jnp.dot(select, repeated, preferred_element_type=jnp.float32).astype(jnp.bfloat16)
    return (placed.reshape(experts, capacity, width), dest)


def body(tokens, expert_ids, w_router, w_gate, w_up, w_down):
    count, width = tokens.shape
    topk = expert_ids.shape[1]
    experts = lax.axis_size("expert") * w_gate.shape[0]
    capacity = 3 * count * topk // (2 * experts)
    groups = lax.axis_size(("pipe", "dp"))
    columns = width // groups
    start = lax.axis_index(("pipe", "dp")) * columns
    mine = lax.dynamic_slice_in_dim(tokens, start, columns, 1)
    local, dest = dispatch(mine, expert_ids, experts, capacity)
    arrived = lax.all_to_all(local, "expert", split_axis=0, concat_axis=0, tiled=True)
    arrived = arrived.reshape(experts * capacity, columns)
    inputs = lax.all_gather(arrived, ("pipe", "dp"), axis=1, tiled=True)
    gate = jnp.dot(inputs, w_gate[0], preferred_element_type=jnp.float32)
    upper = jnp.dot(inputs, w_up[0], preferred_element_type=jnp.float32)
    hidden = (jax.nn.silu(gate) * upper).astype(jnp.bfloat16)
    term = jnp.dot(hidden, w_down[0], preferred_element_type=jnp.float32).astype(jnp.bfloat16)
    logits = jnp.dot(tokens, w_router, preferred_element_type=jnp.float32)
    chosen = jnp.take_along_axis(logits, expert_ids, axis=1)
    first = jax.nn.sigmoid(chosen[:, 0] - chosen[:, 1])
    gates = jnp.stack([first, 1.0 - first], axis=1)
    summed = lax.psum_scatter(term, ("pipe", "dp"), scatter_dimension=1, tiled=True)
    returned = lax.all_to_all(
        summed.reshape(experts, capacity, columns),
        "expert",
        split_axis=0,
        concat_axis=0,
        tiled=True,
    )
    picked = jnp.take(returned.reshape(experts * capacity, columns), dest, axis=0)
    picked = picked.reshape(count, topk, columns).astype(jnp.float32)
    return jnp.sum(gates[:, :, None] * picked, axis=1).astype(jnp.bfloat16)


def solution(mesh):
    placed = (
        P("expert", None),
        P("expert", None),
        P(),
        P("expert", None, ("pipe", "dp")),
        P("expert", None, ("pipe", "dp")),
        P("expert", ("pipe", "dp"), None),
    )
    return jax.shard_map(
        body, mesh=mesh, in_specs=placed, out_specs=P("expert", ("pipe", "dp")), check_vma=False
    )
```

profile of v0, /device:TPU:1, one launch (start us, length us, event | category | flops | bytes accessed | tf_op | source)
XLA Modules:
  0.0 195.6 jit_solution(6473342927977986380)
XLA Ops:
  6.5 0.0 copy-start
  6.5 0.0 all-gather.2.cloned.1.call-start
  6.5 0.9 copy.45
  7.5 0.1 eq.40
  7.6 0.0 copy-start.5
  7.7 0.6 reduce-window.6
  8.2 0.8 slice_reduce_fusion
  9.0 0.0 copy-done.5
  9.0 0.9 constant_dynamic-slice_fusion
  9.9 0.1 broadcast_in_dim.23
  10.1 0.1 reshape.198
  10.1 0.7 reduce-window.9
  10.9 0.1 copy.48
  10.9 0.1 broadcast.109
  11.0 0.7 fusion.20
  11.8 0.6 copy-done.3
  12.3 0.7 multiply_add_fusion
  13.0 0.3 convolution_convert_fusion.1
  13.3 15.7 %all_to_all.10 = bf16[16,24,384]{2,1,0:T(8,128)(2,1)} all-to-all(bf16[16,24,384]{2,1,0:T(8,128)(2,1)S(1)} %bitcast.50), channel_id=1, replica_groups=mesh['pipe'=2,'expert'=16,'dp'=8] {'expert'}, dimensions={0} | all-to-all | bytes 589824 | tf_op jit(solution)/shard_map/all_to_all | solution.py:41
  28.9 0.0 all-gather.2.cloned.1.call-update
  29.0 0.0 reduce-scatter.4.cloned.1.call-start
  29.0 43.7 %all-gather.2.cloned.1.call-done = bf16[384,6144]{1,0:T(8,128)(2,1)} async-done(((bf16[384,384]{1,0:T(8,128)(2,1)}), bf16[384,6144]{1,0:T(8,128)(2,1)}) %all-gather.2.cloned.1.call-update) | async-done | bytes 4718608 | tf_op jit(solution)/shard_map/all_gather | solution.py:43
  72.8 4.7 %fusion.3 = f32[384,256]{1,0:T(8,128)S(1)} fusion(bf16[384,6144]{1,0:T(8,128)(2,1)} %all-gather.2.cloned.1.call-done, bf16[1,6144,256]{2,1,0:T(8,128)(2,1)} %param.9), kind=kOutput, calls=%fused_computation.6 | convolution fusion | flops 1207959552 | bytes 8257536 | tf_op jit(solution)/shard_map/dot_general | solution.py:44
  77.5 0.0 copy-done
  77.5 10.6 %convolution_convert_fusion = bf16[384,6144]{1,0:T(8,128)(2,1)} fusion(bf16[1,256,6144]{2,1,0:T(8,128)(2,1)S(1)} %copy-done, bf16[384,6144]{1,0:T(8,128)(2,1)} %all-gather.2.cloned.1.call-done, bf16[1,6144,256]{2,1,0:T(8,128)(2,1)} %param.10, f32[384,256]{1,0:T(8,128)S(1)} %fusion.3), kind=kOutput, calls=%fused_computation.2 | convolution fusion | flops 2418868224 | bytes 16121856 | tf_op jit(solution)/shard_map/dot_general | solution.py:47
  88.0 6.6 %copy.52 = bf16[384,6144]{0,1:T(8,128)(2,1)} copy(bf16[384,6144]{1,0:T(8,128)(2,1)} %convolution_convert_fusion) | data formatting | bytes 9437184
  94.7 0.0 reduce-scatter.4.cloned.1.call-update
  94.7 0.6 copy-done.4
  95.3 0.1 reduce_sum.23
  95.5 0.0 copy-done.2
  95.5 0.1 copy.51
  95.6 0.1 mul.61
  95.7 0.1 copy.49
  95.8 0.1 copy.50
  96.0 0.1 copy.42
  96.1 0.1 reshape.211
  96.3 1.9 fusion.22
  98.2 2.0 %gather_fusion.1 = f32[256]{0:T(256)S(1)} fusion(f32[128,16]{0,1:T(8,128)S(1)} %fusion.22, s32[256]{0:T(256)S(1)} %reshape.211), kind=kCustom, calls=%fused_computation.1 | custom fusion | bytes 4096 | tf_op jit(solution)/shard_map/jit(take_along_axis)/gather | solution.py:49
  100.2 0.1 reshape.214
  100.3 0.1 copy.43
  100.4 0.1 copy.44
  100.5 67.4 %reduce-scatter.4.cloned.1.call-done = bf16[384,384]{1,0:T(8,128)(2,1)} async-done(((bf16[6144,384]{1,0:T(8,128)(2,1)}), bf16[384,384]{1,0:T(8,128)(2,1)}) %reduce-scatter.4.cloned.1.call-update) | async-done | bytes 294928
  168.0 1.8 copy.53
  169.8 6.3 %all-to-all-start.1 = ((bf16[16,24,384]{2,1,0:T(8,128)(2,1)}), bf16[16,24,384]{2,1,0:T(8,128)(2,1)S(1)}, u32[]{:S(2)}, u32[]{:S(2)}) async-start(bf16[16,24,384]{2,1,0:T(8,128)(2,1)} %bitcast.49), calls=%async_computation.1 | async-start | bytes 589824 | tf_op jit(solution)/shard_map/all_to_all | solution.py:53
  176.2 8.5 %all-to-all-done.1 = bf16[16,24,384]{2,1,0:T(8,128)(2,1)S(1)} async-done(((bf16[16,24,384]{2,1,0:T(8,128)(2,1)}), bf16[16,24,384]{2,1,0:T(8,128)(2,1)S(1)}, u32[]{:S(2)}, u32[]{:S(2)}) %all-to-all-start.1) | async-done | bytes 294944 | tf_op jit(solution)/shard_map/all_to_all | solution.py:53
  184.6 1.8 gather_fusion
  186.5 1.0 gather.12
  187.5 1.3 multiply_reduce_fusion
  (17 shorter events, 0.1 us)
Async XLA Ops:
  6.5 70.9 %copy-start = (bf16[1,256,6144]{2,1,0:T(8,128)(2,1)S(1)}, bf16[1,256,6144]{2,1,0:T(8,128)(2,1)}, u32[]{:S(2)}) copy-start(bf16[1,256,6144]{2,1,0:T(8,128)(2,1)} %param.11) | copy-start | bytes 9437188
  6.5 66.2 %all-gather.2.cloned.1.call-start = ((), (), s32[]{:S(2)}) async-start(), calls=%async_computation.3 | async-start | bytes 5013504 | tf_op jit(solution)/shard_map/all_gather | solution.py:43
  7.6 1.4 copy-start.5
  11.8 0.6 copy-start.3
  29.0 139.0 %reduce-scatter.4.cloned.1.call-start = ((), (), s32[]{:S(2)}) async-start(), calls=%async_computation.4 | async-start | bytes 5013504
  94.7 0.7 copy-start.4
  94.7 0.8 copy-start.2
  94.7 1.6 copy-start.1
  169.8 14.8 %all-to-all-start.1 = ((bf16[16,24,384]{2,1,0:T(8,128)(2,1)}), bf16[16,24,384]{2,1,0:T(8,128)(2,1)S(1)}, u32[]{:S(2)}, u32[]{:S(2)}) async-start(bf16[16,24,384]{2,1,0:T(8,128)(2,1)} %bitcast.49), calls=%async_computation.1 | async-start | bytes 589824 | tf_op jit(solution)/shard_map/all_to_all | solution.py:53
Sparse Core Ops, SparseCore 0:
  29.1 43.6 all-gather.1
  94.8 73.1 reduce-scatter.3
where the time goes:
time: 196 us
  waiting for transfers between devices  120 us (61%)
  local copies, waits for them, and re-layouts  18.7 us (10%)
  matrix products  17.4 us (9%)
  blocking collectives  15.7 us (8%)
  between operations  13.6 us (7%)
  starting transfers between devices  6.36 us (3%)
  other arithmetic  4.13 us (2%)
    unnamed x3, waiting for transfers between devices  67.5 us
    all_gather x1, waiting for transfers between devices, body(): inputs = lax.all_gather(arrived, ('pipe', 'dp'), axis=1, tiled=True)  43.7 us
    all_to_all x1, blocking collectives, body(): lax.all_to_all(local, 'expert', split_axis=0, concat_axis=0, tiled=True)  15.7 us
    unnamed x15, local copies, waits for them, and re-layouts  10.6 us
    dot_general x1, matrix products, body(): jnp.dot(hidden, w_down[0], preferred_element_type=jnp.float32)  10.6 us
    all_to_all x1, waiting for transfers between devices, body(): lax.all_to_all(summed.reshape(experts, capacity, columns), 'expert', spli...  8.47 us
    all_to_all x1, starting transfers between devices, body(): lax.all_to_all(summed.reshape(experts, capacity, columns), 'expert', spli...  6.32 us
    dot_general x1, matrix products, body(): gate = jnp.dot(inputs, w_gate[0], preferred_element_type=jnp.float32)  4.71 us
  transfers between devices with their start and end apart: 3, of which 3 were waited for; matrix products, arithmetic and copies ran while one was open for 3% of the time, Pallas kernels for 0%

commit v1 on v0

--- a/solution.py
+++ b/solution.py
@@ -40,7 +40,12 @@
     local, dest = dispatch(mine, expert_ids, experts, capacity)
     arrived = lax.all_to_all(local, "expert", split_axis=0, concat_axis=0, tiled=True)
     arrived = arrived.reshape(experts * capacity, columns)
-    inputs = lax.all_gather(arrived, ("pipe", "dp"), axis=1, tiled=True)
+    inputs = jnp.concatenate(
+        lax.all_to_all(
+            jnp.stack([arrived] * lax.axis_size(("pipe", "dp")), 0), ("pipe", "dp"), 0, 0
+        ),
+        1,
+    )
     gate = jnp.dot(inputs, w_gate[0], preferred_element_type=jnp.float32)
     upper = jnp.dot(inputs, w_up[0], preferred_element_type=jnp.float32)
     hidden = (jax.nn.silu(gate) * upper).astype(jnp.bfloat16)

time: 196 us -> 258 us (1.32)
  blocking collectives: 15.7 us -> 130 us
  waiting for transfers between devices: 120 us -> 72.9 us
  matrix products: 17.4 us -> 8.62 us
    all_to_all x0 -> x1, blocking collectives: none -> 115 us  [body(): lax.all_to_all(jnp.stack([arrived] * lax.axis_size(('pipe', 'dp')), 0), (...]
    all_gather x1 -> x0, waiting for transfers between devices: 43.7 us -> none  [body(): inputs = lax.all_gather(arrived, ('pipe', 'dp'), axis=1, tiled=True)]
    dot_general x1, matrix products: 10.6 us -> 3.59 us  [body(): jnp.dot(hidden, w_down[0], preferred_element_type=jnp.float32)]
    dot_general x1, matrix products: 4.71 us -> 1.42 us  [body(): gate = jnp.dot(inputs, w_gate[0], preferred_element_type=jnp.float32)]
    unnamed x3 -> x2, waiting for transfers between devices: 67.5 us -> 64.7 us
    unnamed x15 -> x19, local copies, waits for them, and re-layouts: 10.6 us -> 11.1 us
  transfers between devices with their start and end apart: 3 -> 2, of which waited for: 3 -> 2; matrix products, arithmetic and copies ran while one was open for 3% -> 2% of each run, Pallas kernels for 0% -> 0%
where the time goes in v1:
time: 258 us; the launch traced here: 257 us
  blocking collectives  130 us (50%)
  waiting for transfers between devices  72.9 us (28%)
  local copies, waits for them, and re-layouts  21 us (8%)
  between operations  13.6 us (5%)
  matrix products  8.62 us (3%)
  starting transfers between devices  6.44 us (2%)
  other arithmetic  4.13 us (2%)
    all_to_all x1, blocking collectives, body(): lax.all_to_all(jnp.stack([arrived] * lax.axis_size(('pipe', 'dp')), 0), (...  115 us
    unnamed x2, waiting for transfers between devices  64.7 us
    all_to_all x1, blocking collectives, body(): lax.all_to_all(local, 'expert', split_axis=0, concat_axis=0, tiled=True)  15.7 us
    unnamed x19, local copies, waits for them, and re-layouts  11.1 us
    all_to_all x1, waiting for transfers between devices, body(): lax.all_to_all(summed.reshape(experts, capacity, columns), 'expert', spli...  8.2 us
    all_to_all x1, starting transfers between devices, body(): lax.all_to_all(summed.reshape(experts, capacity, columns), 'expert', spli...  6.44 us
  transfers between devices with their start and end apart: 2, of which 2 were waited for; matrix products, arithmetic and copies ran while one was open for 2% of the time, Pallas kernels for 0%

profile of v1, /device:TPU:1, one launch (start us, length us, event | category | flops | bytes accessed | tf_op | source)
XLA Modules:
  0.0 257.0 jit_solution(4475885248191338239)
XLA Ops:
  6.5 0.0 copy-start
  6.5 0.0 reduce-scatter.4.cloned.1.call-start
  6.5 0.9 copy.48
  7.5 0.1 eq.40
  7.7 0.6 reduce-window.6
  8.2 0.8 slice_reduce_fusion
  9.0 0.9 constant_dynamic-slice_fusion
  9.9 0.1 broadcast_in_dim.23
  10.1 0.1 reshape.203
  10.1 0.7 reduce-window.9
  10.9 0.1 copy.51
  10.9 0.1 broadcast.110
  11.0 0.7 fusion.12
  11.8 0.6 copy-done.5
  12.3 0.7 multiply_add_fusion
  13.0 0.3 convolution_convert_fusion.1
  13.3 15.7 %all_to_all.15 = bf16[16,24,384]{2,1,0:T(8,128)(2,1)} all-to-all(bf16[16,24,384]{2,1,0:T(8,128)(2,1)S(1)} %bitcast.54), channel_id=1, replica_groups=mesh['pipe'=2,'expert'=16,'dp'=8] {'expert'}, dimensions={0} | all-to-all | bytes 589824 | tf_op jit(solution)/shard_map/all_to_all | solution.py:41
  28.9 1.2 copy.54
  30.1 0.6 stack.9
  30.7 0.0 copy-start.1
  30.7 114.7 %all_to_all.16 = bf16[16,384,384]{1,2,0:T(8,128)(2,1)S(1)} all-to-all(bf16[16,384,384]{1,2,0:T(8,128)(2,1)S(1)} %stack.9), channel_id=1, replica_groups=mesh['pipe'=2,'expert'=16,'dp'=8] {'pipe','dp'}, dimensions={0} | all-to-all | bytes 9437184 | tf_op jit(solution)/shard_map/all_to_all | solution.py:44
  145.4 1.4 fusion.3
  146.8 0.5 copy-done.2
  147.3 1.4 fusion.8
  148.7 0.0 copy-done
  148.7 3.6 %convolution_convert_fusion = bf16[384,6144]{1,0:T(8,128)(2,1)} fusion(bf16[384,256]{1,0:T(8,128)(2,1)S(1)} %fusion.8, bf16[1,256,6144]{2,1,0:T(8,128)(2,1)S(1)} %copy-done), kind=kOutput, calls=%fused_computation.2 | convolution fusion | flops 1210318848 | bytes 8060928 | tf_op jit(solution)/shard_map/dot_general | solution.py:52
  152.3 6.6 %copy.56 = bf16[384,6144]{0,1:T(8,128)(2,1)} copy(bf16[384,6144]{1,0:T(8,128)(2,1)} %convolution_convert_fusion) | data formatting | bytes 9437184
  159.0 0.0 reduce-scatter.4.cloned.1.call-update
  159.0 0.6 copy-done.6
  159.6 0.1 reduce_sum.23
  159.8 0.1 copy.55
  159.9 0.1 mul.61
  160.0 0.1 copy.52
  160.1 0.1 copy.53
  160.3 0.1 copy.45
  160.4 0.1 reshape.217
  160.6 1.9 fusion.13
  162.5 2.0 gather_fusion.1
  164.5 0.1 reshape.220
  164.6 0.1 copy.46
  164.7 0.1 copy.47
  164.8 64.7 %reduce-scatter.4.cloned.1.call-done = bf16[384,384]{1,0:T(8,128)(2,1)} async-done(((bf16[6144,384]{1,0:T(8,128)(2,1)}), bf16[384,384]{1,0:T(8,128)(2,1)}) %reduce-scatter.4.cloned.1.call-update) | async-done | bytes 294928
  229.5 1.8 copy.57
  231.4 6.4 %all-to-all-start.2 = ((bf16[16,24,384]{2,1,0:T(8,128)(2,1)}), bf16[16,24,384]{2,1,0:T(8,128)(2,1)S(1)}, u32[]{:S(2)}, u32[]{:S(2)}) async-start(bf16[16,24,384]{2,1,0:T(8,128)(2,1)} %bitcast.52), calls=%async_computation.2 | async-start | bytes 589824 | tf_op jit(solution)/shard_map/all_to_all | solution.py:58
  237.9 8.2 %all-to-all-done.2 = bf16[16,24,384]{2,1,0:T(8,128)(2,1)S(1)} async-done(((bf16[16,24,384]{2,1,0:T(8,128)(2,1)}), bf16[16,24,384]{2,1,0:T(8,128)(2,1)S(1)}, u32[]{:S(2)}, u32[]{:S(2)}) %all-to-all-start.2) | async-done | bytes 294944 | tf_op jit(solution)/shard_map/all_to_all | solution.py:58
  246.1 1.8 gather_fusion
  247.9 1.0 gather.12
  248.9 1.3 multiply_reduce_fusion
  (22 shorter events, 0.1 us)
Async XLA Ops:
  6.5 142.2 %copy-start = (bf16[1,256,6144]{2,1,0:T(8,128)(2,1)S(1)}, bf16[1,256,6144]{2,1,0:T(8,128)(2,1)}, u32[]{:S(2)}) copy-start(bf16[1,256,6144]{2,1,0:T(8,128)(2,1)} %param.11) | copy-start | bytes 9437188
  6.5 223.0 %reduce-scatter.4.cloned.1.call-start = ((), (), s32[]{:S(2)}) async-start(), calls=%async_computation.4 | async-start | bytes 5013504
  7.6 1.4 copy-start.7
  11.8 0.6 copy-start.5
  30.7 114.7 %copy-start.1 = (bf16[1,6144,256]{2,1,0:T(8,128)(2,1)S(1)}, bf16[1,6144,256]{2,1,0:T(8,128)(2,1)}, u32[]{:S(2)}) copy-start(bf16[1,6144,256]{2,1,0:T(8,128)(2,1)} %param.9) | copy-start | bytes 9437188
  145.4 1.9 copy-start.2
  159.0 0.7 copy-start.6
  159.0 0.8 copy-start.4
  159.0 1.6 copy-start.3
  231.4 14.7 %all-to-all-start.2 = ((bf16[16,24,384]{2,1,0:T(8,128)(2,1)}), bf16[16,24,384]{2,1,0:T(8,128)(2,1)S(1)}, u32[]{:S(2)}, u32[]{:S(2)}) async-start(bf16[16,24,384]{2,1,0:T(8,128)(2,1)} %bitcast.52), calls=%async_computation.2 | async-start | bytes 589824 | tf_op jit(solution)/shard_map/all_to_all | solution.py:58
Sparse Core Ops, SparseCore 0:
  159.1 70.3 reduce-scatter.3
